TPU v7x, 256 devices: a whole 4x4x8 slice. The times are simulated.
256 devices in a mesh: tm: 32 (over z, x), region: 8 (over y, core).
Axes of the slice: x: 4, y: 4, z: 8, core: 2. Of those that a mesh axis runs over, the one named last changes fastest.
Arguments:
- start_primal: float32 [2048, 8, 3200], P('tm', 'region'), may hold values from 0 to 10, as said below
- demand: float32 [2048, 8, 3200], P('tm', 'region'), may hold values from -30 to 30
- unit_cost: float32 [8, 3200], P('region'), may hold values from -5 to 5
- build_cost: float32 [8, 128], P('region', 'tm'), may hold values from 0.5 to 2
- start_capacity: float32 [8, 128], P('region', 'tm'), may hold values from 0 to 2
- net_weights: float32 [8, 25, 3, 128, 128], P('region'), may hold values from -0.3125 to 0.3125
- net_columns: int32 [8, 25, 3], P('region'), may hold values from 0 to 24
- line_weights: float32 [8, 4, 128, 128], P('region'), may hold values from -0.25 to 0.25
- line_source: int32 [8, 4], replicated, may hold values from 0 to 7
- generator_map: int32 [8, 128], P('region'), may hold values from 0 to 127
Outputs:
- primal_final: float32 [2048, 8, 3200], P('tm', 'region')
- dual_final: float32 [2048, 8, 3200], P('tm', 'region')
- capacity_final: float32 [8, 128], P('region', 'tm')
Inputs may be any that keep to these rules, and one draw needn't show every extreme that they name: `start_primal`: Nonnegative.
All inputs are finite; a program needn't handle non-finite values.
Results may differ from a plain program's by a relative error of at most 0.0003.
Values sent between devices are 32-bit elements; how exact they have to be, the bound alone decides.
A program may use at most 64 MiB of HBM per device.

v0:
```python
import math
import jax
import jax.numpy as jnp
from jax import lax
from jax.sharding import PartitionSpec as P

ITERS = 4
HIGHEST_PRECISION = lax.Precision.HIGHEST
STEP_SCALE = 0.2
EPSILON = 1e-06


def shifted(shard, axis, by):
    devices = lax.axis_size(axis)
    pairs = [(i, i + by) for i in range(devices) if 0 <= i + by < devices]
    return lax.ppermute(shard, axis, pairs)


def network_forward(blocks, weights, columns):
    hour_count = blocks.shape[0]
    picked = jnp.take(blocks, columns.reshape(-1), axis=1)
    flat_weights = weights.reshape(-1, weights.shape[2], weights.shape[3])
    product = jnp.einsum("hpk,pkl->hpl", picked, flat_weights, precision=HIGHEST_PRECISION)
    return product.reshape(hour_count, columns.shape[0], columns.shape[1], -1).sum(axis=2)


def network_adjoint(dual_rows, weights, columns):
    hour_count = dual_rows.shape[0]
    partial_value = jnp.einsum("hil,iskl->hisk", dual_rows, weights, precision=HIGHEST_PRECISION)
    block_count = columns.shape[0]
    placing = (columns.reshape(-1)[:, None] == jnp.arange(block_count)[None, :]).astype(jnp.float32)
    stacked = partial_value.reshape(hour_count, -1, partial_value.shape[3])
    return jnp.einsum("hpk,pc->hck", stacked, placing, precision=HIGHEST_PRECISION)


def body(
    start_primal,
    demand,
    unit_cost,
    build_cost,
    start_capacity,
    net_weights,
    net_columns,
    line_weights,
    line_source,
    generator_map,
):
    hour_count, _, row_width = start_primal.shape
    block_size = net_weights.shape[3]
    block_count = row_width // block_size
    tm_count = lax.axis_size("tm")
    region_count = lax.axis_size("region")
    own_region = lax.axis_index("region")
    weights = net_weights[0]
    columns = net_columns[0]
    line_mats = line_weights[0]
    unit_rows = unit_cost.reshape(block_count, block_size)
    invest_own = start_capacity.shape[1]
    invest_all = invest_own * tm_count
    couple = 1.0 / math.sqrt(hour_count * tm_count)
    primal_count = hour_count * tm_count * region_count * row_width + region_count * invest_all
    dual_count = hour_count * tm_count * region_count * row_width
    selector = (generator_map[0][:, None] == jnp.arange(invest_all)[None, :]).astype(jnp.float32)
    line_links = (line_source[:, :, None] == jnp.arange(region_count)[None, None, :]).astype(
        jnp.float32
    )
    own_sources = lax.dynamic_index_in_dim(line_links, own_region, 0, keepdims=False)
    free_column = (jnp.arange(block_count) == 3)[None, :, None]
    free_row = (jnp.arange(block_count) < 3)[None, :, None]
    primal = start_primal.reshape(hour_count, block_count, block_size)
    target = demand.reshape(hour_count, block_count, block_size)
    dual = jnp.zeros_like(primal)
    primal_weight = jnp.float32(1.0)
    capacity, build_rows = (
        lax.all_gather(start_capacity[0], "tm", axis=0, tiled=True),
        lax.all_gather(build_cost[0], "tm", axis=0, tiled=True),
    )
    for iteration in range(ITERS):
        primal_step = STEP_SCALE / primal_weight
        dual_step = STEP_SCALE * primal_weight
        adjoint = network_adjoint(dual, weights, columns)
        after = shifted(dual[0, 0], "tm", -1)
        following = jnp.concatenate([dual[1:, 0], after[None]], axis=0)
        partial_lines = jnp.einsum(
            "hl,jkl->jhk", dual[:, 1], line_mats, precision=HIGHEST_PRECISION
        )
        line_back = lax.psum_scatter(
            jnp.einsum("jq,jhk->qhk", own_sources, partial_lines, precision=HIGHEST_PRECISION),
            "region",
            scatter_dimension=0,
            tiled=True,
        )[0]
        adjoint = adjoint.at[:, 0].add(-following).at[:, 3].add(line_back)
        column_sums = jnp.sum(dual[:, 2], axis=0)
        capacity_part = couple * jnp.dot(column_sums, selector, precision=HIGHEST_PRECISION)
        moved = primal - primal_step * (unit_rows[None] - adjoint)
        new_primal = jnp.where(free_column, moved, jnp.maximum(moved, 0.0))
        capacity_grad = lax.psum(capacity_part, "tm")
        new_capacity = jnp.maximum(capacity - primal_step * (build_rows - capacity_grad), 0.0)
        capacity_bar = 2.0 * new_capacity - capacity
        capacity_change = lax.dynamic_slice_in_dim(
            new_capacity - capacity, lax.axis_index("tm") * invest_own, invest_own, 0
        )
        primal_bar = 2.0 * new_primal - primal
        primal_local = jnp.sum((new_primal - primal) ** 2) + jnp.sum(capacity_change**2)
        if iteration + 1 < ITERS:
            primal_total = lax.psum(primal_local, ("tm", "region"))
        applied = network_forward(primal_bar, weights, columns)
        before = shifted(primal_bar[-1, 0], "tm", 1)
        earlier = jnp.concatenate([before[None], primal_bar[:-1, 0]], axis=0)
        chosen_flows = jnp.einsum(
            "jr,rhk->jhk",
            own_sources,
            lax.all_gather(primal_bar[:, 3][None], "region", axis=0, tiled=True),
            precision=HIGHEST_PRECISION,
        )
        line_flow = jnp.einsum("jhk,jkl->hl", chosen_flows, line_mats, precision=HIGHEST_PRECISION)
        picked_capacity = jnp.dot(selector, capacity_bar, precision=HIGHEST_PRECISION)
        applied = (
            applied.at[:, 0]
            .add(-earlier)
            .at[:, 1]
            .add(line_flow)
            .at[:, 2]
            .add(couple * picked_capacity[None])
        )
        moved_dual = dual + dual_step * (target - applied)
        new_dual = jnp.where(free_row, moved_dual, jnp.maximum(moved_dual, 0.0))
        if iteration + 1 < ITERS:
            dual_local = jnp.sum((new_dual - dual) ** 2)
            dual_total = lax.psum(dual_local, ("tm", "region"))
            primal_weight = jnp.sqrt(
                primal_weight
                * jnp.sqrt(primal_total / primal_count + EPSILON)
                / jnp.sqrt(dual_total / dual_count + EPSILON)
            )
        primal, dual, capacity = (new_primal, new_dual, new_capacity)
    capacity_own = lax.dynamic_slice_in_dim(
        capacity, lax.axis_index("tm") * invest_own, invest_own, 0
    )
    return (
        primal.reshape(hour_count, 1, row_width),
        dual.reshape(hour_count, 1, row_width),
        capacity_own[None],
    )


def solution(mesh):
    in_specs = (
        P("tm", "region", None),
        P("tm", "region", None),
        P("region", None),
        P("region", "tm"),
        P("region", "tm"),
        P("region", None, None, None, None),
        P("region", None, None),
        P("region", None, None, None),
        P(),
        P("region", None),
    )
    out_specs = (P("tm", "region", None), P("tm", "region", None), P("region", "tm"))
    return jax.shard_map(body, mesh=mesh, in_specs=in_specs, out_specs=out_specs, check_vma=False)
```

profile of v0, /device:TPU:1, one launch (start us, length us, event | category | flops | bytes accessed | tf_op | source)
XLA Modules:
  0.0 858.2 jit_solution(13189949462657411320)
XLA Ops:
  7.2 1.4 collective-permute-start
  12.9 9.0 %fusion.6 = f32[25,64,3,128]{3,1,2,0:T(8,128)S(1)} fusion(f32[1,25,3,128,128]{4,3,2,1,0:T(8,128)} %param.57), kind=kOutput, calls=%fused_computation.10 | convolution fusion | flops 943718400 | bytes 7372800 | tf_op jit(solution)/shard_map/hil,iskl->hisk/dot_general | solution.py:29
  22.0 2.4 fusion.14
  27.1 76.9 %all-reduce.6 = (f32[128]{0:T(128)S(1)}, f32[128]{0:T(128)S(1)}, f32[128]{0:T(128)S(1)}) all-reduce(f32[128]{0:T(128)S(1)} %bitcast_dynamic-update-slice_fusion.1, f32[128]{0:T(128)S(1)} %bitcast_dynamic-update-slice_fusion, f32[128]{0:T(128)S(1)} %fusion.51), channel_id=2, replica_groups=mesh['tm'=32,'region'=8] {'tm'}, use_global_device_ids=true, to_apply=%add.1 | all-reduce | flops 384 | bytes 3072 | tf_op jit(solution)/shard_map/all_gather | solution.py:75
  104.3 1.9 reduce.45
  106.3 3.1 reduce.43
  113.3 28.2 %all-gather.2 = f32[512,1,128]{2,1,0:T(1,128)S(1)} all-gather(f32[64,1,128]{2,1,0:T(1,128)S(1)} %bitcast.385), channel_id=4, replica_groups=mesh['tm'=32,'region'=8] {'region'}, dimensions={0}, use_global_device_ids=true | all-gather | bytes 294912 | tf_op jit(solution)/shard_map/all_gather | solution.py:114
  141.5 2.1 gather_fusion
  143.6 7.9 fusion.22
  153.2 2.0 reduce_sum.150
  157.0 10.5 %fusion.4 = f32[25,64,3,128]{3,1,2,0:T(8,128)} fusion(f32[1,25,3,128,128]{4,3,2,1,0:T(8,128)} %param.57, f32[64,25,128]{2,0,1:T(8,128)S(1)} %get-tuple-element.281), kind=kOutput, calls=%fused_computation.8 | convolution fusion | flops 943718400 | bytes 8192000 | tf_op jit(solution)/shard_map/hil,iskl->hisk/dot_general | solution.py:29
  167.7 55.8 %psum.73 = f32[128]{0:T(128)S(1)} all-reduce(f32[128]{0:T(128)S(1)} %fusion.49), channel_id=1, replica_groups=mesh['tm'=32,'region'=8] {'tm'}, use_global_device_ids=true, to_apply=%region_11.13 | all-reduce | flops 128 | bytes 1024 | tf_op jit(solution)/shard_map/psum | solution.py:98
  223.5 89.7 %all-reduce.5 = (f32[]{:T(128)}, f32[]{:T(128)}) all-reduce(f32[]{:T(128)S(6)} %add.249, f32[]{:T(128)} %get-tuple-element.280), channel_id=1, replica_groups=mesh['tm'=32,'region'=8] {'tm','region'}, use_global_device_ids=true, to_apply=%region_4.5 | all-reduce | flops 2 | bytes 16 | tf_op jit(solution)/shard_map/psum | solution.py:107
  317.6 4.0 fusion.12
  325.8 22.6 %reduce-scatter.7.cloned.1.call-done = f32[1,64,128]{2,1,0:T(8,128)} async-done(((f32[8,64,128]{2,1,0:T(8,128)}), f32[1,64,128]{2,1,0:T(8,128)}) %reduce-scatter.7.cloned.1.call-update) | async-done | bytes 32784 | tf_op jit(solution)/shard_map/reduce_scatter | solution.py:87
  348.4 1.4 fusion.106
  349.7 2.2 multiply_reduce_fusion.3
  352.8 2.1 gather_fusion.1
  354.9 2.8 collective-permute-start.3
  357.8 16.1 %all-gather.3 = f32[512,1,128]{2,1,0:T(1,128)S(1)} all-gather(f32[64,1,128]{2,1,0:T(1,128)S(1)} %bitcast.383), channel_id=5, replica_groups=mesh['tm'=32,'region'=8] {'region'}, dimensions={0}, use_global_device_ids=true | all-gather | bytes 294912 | tf_op jit(solution)/shard_map/all_gather | solution.py:114
  373.9 7.9 fusion.20
  383.4 2.0 reduce_sum.155
  387.2 10.5 %fusion.2 = f32[25,64,3,128]{3,1,2,0:T(8,128)} fusion(f32[1,25,3,128,128]{4,3,2,1,0:T(8,128)} %param.57, f32[64,25,128]{2,0,1:T(8,128)S(1)} %get-tuple-element.275), kind=kOutput, calls=%fused_computation.6 | convolution fusion | flops 943718400 | bytes 8192000 | tf_op jit(solution)/shard_map/hil,iskl->hisk/dot_general | solution.py:29
  397.9 59.1 %psum.76 = f32[128]{0:T(128)S(1)} all-reduce(f32[128]{0:T(128)S(1)} %fusion.47), channel_id=1, replica_groups=mesh['tm'=32,'region'=8] {'tm'}, use_global_device_ids=true, to_apply=%region_20.22 | all-reduce | flops 128 | bytes 1024 | tf_op jit(solution)/shard_map/psum | solution.py:98
  457.0 86.0 %all-reduce.4 = (f32[]{:T(128)}, f32[]{:T(128)}) all-reduce(f32[]{:T(128)S(6)} %add.257, f32[]{:T(128)} %get-tuple-element.274), channel_id=1, replica_groups=mesh['tm'=32,'region'=8] {'tm','region'}, use_global_device_ids=true, to_apply=%region_13.15 | all-reduce | flops 2 | bytes 16 | tf_op jit(solution)/shard_map/psum | solution.py:107
  547.2 4.0 fusion.10
  555.4 23.9 %reduce-scatter.9.cloned.1.call-done = f32[1,64,128]{2,1,0:T(8,128)} async-done(((f32[8,64,128]{2,1,0:T(8,128)}), f32[1,64,128]{2,1,0:T(8,128)}) %reduce-scatter.9.cloned.1.call-update) | async-done | bytes 32784 | tf_op jit(solution)/shard_map/reduce_scatter | solution.py:87
  580.7 2.2 multiply_reduce_fusion.1
  582.9 2.1 gather_fusion.2
  585.1 2.8 collective-permute-start.5
  587.9 16.1 %all-gather.4 = f32[512,1,128]{2,1,0:T(1,128)S(1)} all-gather(f32[64,1,128]{2,1,0:T(1,128)S(1)} %bitcast.384), channel_id=6, replica_groups=mesh['tm'=32,'region'=8] {'region'}, dimensions={0}, use_global_device_ids=true | all-gather | bytes 294912 | tf_op jit(solution)/shard_map/all_gather | solution.py:114
  604.0 7.9 fusion.18
  613.6 2.0 reduce_sum.160
  615.9 2.2 multiply_reduce_fusion
  618.5 10.5 %fusion = f32[25,64,3,128]{3,1,2,0:T(8,128)} fusion(f32[1,25,3,128,128]{4,3,2,1,0:T(8,128)} %param.57, f32[64,25,128]{2,0,1:T(8,128)S(1)} %get-tuple-element.271), kind=kOutput, calls=%fused_computation.4 | convolution fusion | flops 943718400 | bytes 8192000 | tf_op jit(solution)/shard_map/hil,iskl->hisk/dot_general | solution.py:29
  629.2 59.1 %psum.79 = f32[128]{0:T(128)S(1)} all-reduce(f32[128]{0:T(128)S(1)} %fusion.45), channel_id=1, replica_groups=mesh['tm'=32,'region'=8] {'tm'}, use_global_device_ids=true, to_apply=%region_29.31 | all-reduce | flops 128 | bytes 1024 | tf_op jit(solution)/shard_map/psum | solution.py:98
  688.3 86.0 %all-reduce.3 = (f32[]{:T(128)}, f32[]{:T(128)}) all-reduce(f32[]{:T(128)S(6)} %add.266, f32[]{:T(128)} %get-tuple-element.270), channel_id=1, replica_groups=mesh['tm'=32,'region'=8] {'tm','region'}, use_global_device_ids=true, to_apply=%region_22.24 | all-reduce | flops 2 | bytes 16 | tf_op jit(solution)/shard_map/psum | solution.py:107
  775.8 1.5 collective-permute-start.6
  778.5 4.0 fusion.8
  786.6 24.2 %reduce-scatter.11.cloned.1.call-done = f32[1,64,128]{2,1,0:T(8,128)} async-done(((f32[8,64,128]{2,1,0:T(8,128)}), f32[1,64,128]{2,1,0:T(8,128)}) %reduce-scatter.11.cloned.1.call-update) | async-done | bytes 32784 | tf_op jit(solution)/shard_map/reduce_scatter | solution.py:87
  812.2 2.7 multiply_subtract_fusion
  814.9 2.2 gather_fusion.3
  817.0 2.8 collective-permute-start.7
  819.9 16.1 %all-gather.5 = f32[512,1,128]{2,1,0:T(1,128)S(1)} all-gather(f32[64,1,128]{2,1,0:T(1,128)S(1)} %bitcast.382), channel_id=7, replica_groups=mesh['tm'=32,'region'=8] {'region'}, dimensions={0}, use_global_device_ids=true | all-gather | bytes 294912 | tf_op jit(solution)/shard_map/all_gather | solution.py:114
  836.0 8.0 fusion.16
  844.9 1.7 reshape.912
  846.6 2.0 reduce_sum.162
  849.6 1.7 reshape.913
  (158 shorter events, 41.3 us)
Async XLA Ops:
  7.2 97.1 %copy-start = (f32[64,1,3200]{2,1,0:T(1,128)S(1)}, f32[64,1,3200]{2,1,0:T(1,128)}, u32[]{:S(2)}) copy-start(f32[64,1,3200]{2,1,0:T(1,128)} %param.53) | copy-start | bytes 2457604
  7.2 102.9 %reduce-scatter.5.cloned.1.call-start = ((), (), s32[]{:S(2)}) async-start(), calls=%async_computation.4 | async-start | bytes 294912 | tf_op jit(solution)/shard_map/reduce_scatter | solution.py:87
  7.2 102.8 %collective-permute-start = (f32[128]{0:T(128)S(1)}, f32[128]{0:T(128)S(1)}, u32[]{:S(2)}, u32[]{:S(2)}) collective-permute-start(f32[128]{0:T(128)S(1)} %broadcast.305), channel_id=1, source_target_pairs={{8,0},{16,8},{24,16},{32,24},{40,32},{48,40},{56,48},{64,56},{72,6... | collective-permute-start | bytes 1544 | tf_op jit(solution)/shard_map/ppermute | solution.py:16
  12.0 336.4 %reduce-scatter.7.cloned.1.call-start = ((), (), s32[]{:S(2)}) async-start(), calls=%async_computation.5 | async-start | bytes 294912 | tf_op jit(solution)/shard_map/reduce_scatter | solution.py:87
  24.4 1.0 copy-start.14
  24.4 1.3 copy-start.16
  24.4 2.5 copy-start.12
  24.4 2.6 copy-start.13
  24.4 79.8 %copy-start.11 = (f32[1,3200]{1,0:T(1,128)S(1)}, f32[1,3200]{1,0:T(1,128)}, u32[]{:S(2)}) copy-start(f32[1,3200]{1,0:T(1,128)} %param.54) | copy-start | bytes 38404
  112.0 43.3 %collective-permute-start.1 = (f32[128]{0:T(128)S(1)}, f32[128]{0:T(128)S(1)}, u32[]{:S(2)}, u32[]{:S(2)}) collective-permute-start(f32[128]{0:T(128)S(1)} %slice_bitcast_fusion.16), channel_id=1, source_target_pairs={{0,8},{8,16},{16,24},{24,32},{32,40},{40,48},{48,56},{56,64},{64,7... | collective-permute-start | bytes 1544 | tf_op jit(solution)/shard_map/ppermute | solution.py:16
  151.5 3.8 copy-start.2
  156.6 10.9 %copy-start.8 = (f32[64,25,128]{2,0,1:T(8,128)}, f32[64,25,128]{2,0,1:T(8,128)S(1)}, u32[]{:S(2)}) copy-start(f32[64,25,128]{2,0,1:T(8,128)S(1)} %get-tuple-element.281) | copy-start | bytes 2457604
  167.7 153.9 %copy-start.15 = (s32[1,128]{1,0:T(1,128)S(1)}, s32[1,128]{1,0:T(1,128)}, u32[]{:S(2)}) copy-start(s32[1,128]{1,0:T(1,128)} %param.61) | copy-start | bytes 1540
  314.6 10.5 %collective-permute-start.2 = (f32[128]{0:T(128)S(1)}, f32[128]{0:T(128)S(1)}, u32[]{:S(2)}, u32[]{:S(2)}) collective-permute-start(f32[128]{0:T(128)S(1)} %slice_bitcast_fusion.15), channel_id=1, source_target_pairs={{8,0},{16,8},{24,16},{32,24},{40,32},{48,40},{56,48},{64,56},{72,6... | collective-permute-start | bytes 1544 | tf_op jit(solution)/shard_map/ppermute | solution.py:16
  317.1 262.2 %reduce-scatter.9.cloned.1.call-start = ((), (), s32[]{:S(2)}) async-start(), calls=%async_computation.6 | async-start | bytes 294912 | tf_op jit(solution)/shard_map/reduce_scatter | solution.py:87
  351.9 0.9 copy-start.3
  354.9 30.4 %collective-permute-start.3 = (f32[128]{0:T(128)S(1)}, f32[128]{0:T(128)S(1)}, u32[]{:S(2)}, u32[]{:S(2)}) collective-permute-start(f32[128]{0:T(128)S(1)} %slice_bitcast_fusion.14), channel_id=1, source_target_pairs={{0,8},{8,16},{16,24},{24,32},{32,40},{40,48},{48,56},{56,64},{64,7... | collective-permute-start | bytes 1544 | tf_op jit(solution)/shard_map/ppermute | solution.py:16
  381.8 4.0 copy-start.9
  386.8 10.9 %copy-start.7 = (f32[64,25,128]{2,0,1:T(8,128)}, f32[64,25,128]{2,0,1:T(8,128)S(1)}, u32[]{:S(2)}) copy-start(f32[64,25,128]{2,0,1:T(8,128)S(1)} %get-tuple-element.275) | copy-start | bytes 2457604
  544.5 10.3 %collective-permute-start.4 = (f32[128]{0:T(128)S(1)}, f32[128]{0:T(128)S(1)}, u32[]{:S(2)}, u32[]{:S(2)}) collective-permute-start(f32[128]{0:T(128)S(1)} %slice_bitcast_fusion.13), channel_id=1, source_target_pairs={{8,0},{16,8},{24,16},{32,24},{40,32},{48,40},{56,48},{64,56},{72,6... | collective-permute-start | bytes 1544 | tf_op jit(solution)/shard_map/ppermute | solution.py:16
  547.0 263.9 %reduce-scatter.11.cloned.1.call-start = ((), (), s32[]{:S(2)}) async-start(), calls=%async_computation.7 | async-start | bytes 294912 | tf_op jit(solution)/shard_map/reduce_scatter | solution.py:87
  551.2 29.5 %copy-start.4 = (f32[64,25,128]{2,0,1:T(8,128)S(1)}, f32[64,25,128]{2,0,1:T(8,128)}, u32[]{:S(2)}) copy-start(f32[64,25,128]{2,0,1:T(8,128)} %copy-done.3) | copy-start | bytes 2457604
  585.1 30.5 %collective-permute-start.5 = (f32[128]{0:T(128)S(1)}, f32[128]{0:T(128)S(1)}, u32[]{:S(2)}, u32[]{:S(2)}) collective-permute-start(f32[128]{0:T(128)S(1)} %slice_bitcast_fusion.12), channel_id=1, source_target_pairs={{0,8},{8,16},{16,24},{24,32},{32,40},{40,48},{48,56},{56,64},{64,7... | collective-permute-start | bytes 1544 | tf_op jit(solution)/shard_map/ppermute | solution.py:16
  618.1 10.9 %copy-start.5 = (f32[64,25,128]{2,0,1:T(8,128)}, f32[64,25,128]{2,0,1:T(8,128)S(1)}, u32[]{:S(2)}) copy-start(f32[64,25,128]{2,0,1:T(8,128)S(1)} %get-tuple-element.271) | copy-start | bytes 2457604
  775.8 10.2 %collective-permute-start.6 = (f32[128]{0:T(128)S(1)}, f32[128]{0:T(128)S(1)}, u32[]{:S(2)}, u32[]{:S(2)}) collective-permute-start(f32[128]{0:T(128)S(1)} %slice_bitcast_fusion.11), channel_id=1, source_target_pairs={{8,0},{16,8},{24,16},{32,24},{40,32},{48,40},{56,48},{64,56},{72,6... | collective-permute-start | bytes 1544 | tf_op jit(solution)/shard_map/ppermute | solution.py:16
  817.0 31.6 %collective-permute-start.7 = (f32[128]{0:T(128)S(1)}, f32[128]{0:T(128)S(1)}, u32[]{:S(2)}, u32[]{:S(2)}) collective-permute-start(f32[128]{0:T(128)S(1)} %slice_bitcast_fusion.10), channel_id=1, source_target_pairs={{0,8},{8,16},{16,24},{24,32},{32,40},{40,48},{48,56},{56,64},{64,7... | collective-permute-start | bytes 1544 | tf_op jit(solution)/shard_map/ppermute | solution.py:16
  836.0 8.4 copy-start.10
  844.9 4.1 copy-start.6
  848.9 2.4 copy-start.1
Sparse Core Ops, SparseCore 0:
  12.1 36.2 reduce-scatter.4
  317.2 31.0 reduce-scatter.6
  547.1 32.1 reduce-scatter.8
  778.6 32.1 reduce-scatter.10
where the time goes:
time: 867 us; the launch traced here: 858 us
  blocking collectives  589 us (68%)
  matrix products  94.9 us (11%)
  waiting for transfers between devices  70.8 us (8%)
  other arithmetic  35 us (4%)
  local copies, waits for them, and re-layouts  28.8 us (3%)
  between operations  23.7 us (3%)
  starting transfers between devices  16 us (2%)
    psum x3, blocking collectives, body(): primal_total = lax.psum(primal_local, ('tm', 'region'))  262 us
    psum x3, blocking collectives, body(): capacity_grad = lax.psum(capacity_part, 'tm')  174 us
    all_gather x1, blocking collectives, body(): lax.all_gather(start_capacity[0], 'tm', axis=0, tiled=True)  76.9 us
    all_gather x4, blocking collectives, body(): lax.all_gather(primal_bar[:, 3][None], 'region', axis=0, tiled=True)  76.5 us
    reduce_scatter x4, waiting for transfers between devices, body(): lax.psum_scatter(jnp.einsum('jq,jhk->qhk', own_sources, partial_lines, pr...  70.7 us
    dot_general x4, matrix products, network_adjoint(): jnp.einsum('hil,iskl->hisk', dual_rows, weights, precision=HIGHEST_PRECIS...  40.4 us
    dot_general x4, matrix products, network_forward(): jnp.einsum('hpk,pkl->hpl', picked, flat_weights, precision=HIGHEST_PRECIS...  31.7 us
  transfers between devices with their start and end apart: 12, of which 3 were waited for; matrix products, arithmetic and copies ran while one was open for 11% of the time, Pallas kernels for 0%

commit v1 on v0

--- a/solution.py
+++ b/solution.py
@@ -95,7 +95,11 @@
         capacity_part = couple * jnp.dot(column_sums, selector, precision=HIGHEST_PRECISION)
         moved = primal - primal_step * (unit_rows[None] - adjoint)
         new_primal = jnp.where(free_column, moved, jnp.maximum(moved, 0.0))
-        capacity_grad = lax.psum(capacity_part, "tm")
+        capacity_grad = capacity_part
+        for hop in (1, 2, 4, 8, 16):
+            capacity_grad = capacity_grad + lax.ppermute(
+                capacity_grad, "tm", [(dev, dev ^ hop) for dev in range(32)]
+            )
         new_capacity = jnp.maximum(capacity - primal_step * (build_rows - capacity_grad), 0.0)
         capacity_bar = 2.0 * new_capacity - capacity
         capacity_change = lax.dynamic_slice_in_dim(

time: 867 us -> 699 us (0.81)
  blocking collectives: 589 us -> 375 us
  starting transfers between devices: 16 us -> 59 us
    psum x3 -> x0, blocking collectives: 174 us -> none  [body(): capacity_grad = lax.psum(capacity_part, 'tm')]
    ppermute x0 -> x20, starting transfers between devices: none -> 43.7 us  [body(): lax.ppermute(capacity_grad, 'tm', [(dev, dev ^ hop) for dev in range(32)])]
    psum x3, blocking collectives: 262 us -> 233 us  [body(): primal_total = lax.psum(primal_local, ('tm', 'region'))]
    all_gather x1, blocking collectives: 76.9 us -> 61.3 us  [body(): lax.all_gather(start_capacity[0], 'tm', axis=0, tiled=True)]
    ppermute x0 -> x20, waiting for transfers between devices: none -> 13.7 us  [body(): lax.ppermute(capacity_grad, 'tm', [(dev, dev ^ hop) for dev in range(32)])]
    reduce_scatter x4, waiting for transfers between devices: 70.7 us -> 60.6 us  [body(): lax.psum_scatter(jnp.einsum('jq,jhk->qhk', own_sources, partial_lines, pr...]
  transfers between devices with their start and end apart: 12 -> 32, of which waited for: 3 -> 10; matrix products, arithmetic and copies ran while one was open for 11% -> 14% of each run, Pallas kernels for 0% -> 0%
where the time goes in v1:
time: 699 us; the launch traced here: 688 us
  blocking collectives  375 us (54%)
  matrix products  87.4 us (13%)
  waiting for transfers between devices  74.3 us (11%)
  starting transfers between devices  59 us (8%)
  other arithmetic  37.3 us (5%)
  local copies, waits for them, and re-layouts  31.3 us (4%)
  between operations  23.8 us (3%)
    psum x3, blocking collectives, body(): primal_total = lax.psum(primal_local, ('tm', 'region'))  233 us
    all_gather x4, blocking collectives, body(): lax.all_gather(primal_bar[:, 3][None], 'region', axis=0, tiled=True)  81.2 us
    all_gather x1, blocking collectives, body(): lax.all_gather(start_capacity[0], 'tm', axis=0, tiled=True)  61.3 us
    reduce_scatter x4, waiting for transfers between devices, body(): lax.psum_scatter(jnp.einsum('jq,jhk->qhk', own_sources, partial_lines, pr...  60.6 us
    ppermute x20, starting transfers between devices, body(): lax.ppermute(capacity_grad, 'tm', [(dev, dev ^ hop) for dev in range(32)])  43.7 us
    dot_general x4, matrix products, network_adjoint(): jnp.einsum('hil,iskl->hisk', dual_rows, weights, precision=HIGHEST_PRECIS...  37 us
    dot_general x4, matrix products, network_forward(): jnp.einsum('hpk,pkl->hpl', picked, flat_weights, precision=HIGHEST_PRECIS...  31.7 us
    ppermute x8, starting transfers between devices, shifted(): return lax.ppermute(shard, axis, pairs)  15.1 us
  transfers between devices with their start and end apart: 32, of which 10 were waited for; matrix products, arithmetic and copies ran while one was open for 14% of the time, Pallas kernels for 0%

profile of v1, /device:TPU:1, one launch (start us, length us, event | category | flops | bytes accessed | tf_op | source)
XLA Modules:
  0.0 688.4 jit_solution(3193529362309019845)
XLA Ops:
  9.5 2.7 collective-permute-start.1
  16.5 9.0 %fusion.6 = f32[25,64,3,128]{3,1,2,0:T(8,128)S(1)} fusion(f32[1,25,3,128,128]{4,3,2,1,0:T(8,128)} %param.57), kind=kOutput, calls=%fused_computation.10 | convolution fusion | flops 943718400 | bytes 7372800 | tf_op jit(solution)/shard_map/hil,iskl->hisk/dot_general | solution.py:29
  25.5 2.4 fusion.14
  29.4 3.1 collective-permute-start.2
  33.5 2.4 collective-permute-start.3
  37.1 3.0 collective-permute-start.4
  42.1 3.1 reduce.43
  45.2 61.3 %all-reduce.6 = (f32[128]{0:T(128)S(1)}, f32[128]{0:T(128)S(1)}) all-reduce(f32[128]{0:T(128)S(1)} %bitcast_dynamic-update-slice_fusion.1, f32[128]{0:T(128)S(1)} %bitcast_dynamic-update-slice_fusion), channel_id=2, replica_groups=mesh['tm'=32,'region'=8] {'tm'}, use_global_device_ids=true, to_apply=%add.1 | all-reduce | flops 256 | bytes 2048 | tf_op jit(solution)/shard_map/all_gather | solution.py:75
  106.5 2.4 collective-permute-start.5
  108.9 4.0 collective-permute-done.5
  117.1 32.1 %all-gather.2 = f32[512,1,128]{2,1,0:T(1,128)S(1)} all-gather(f32[64,1,128]{2,1,0:T(1,128)S(1)} %bitcast.388), channel_id=4, replica_groups=mesh['tm'=32,'region'=8] {'region'}, dimensions={0}, use_global_device_ids=true | all-gather | bytes 294912 | tf_op jit(solution)/shard_map/all_gather | solution.py:118
  151.3 7.9 %fusion.22 = f32[75,64,128]{2,1,0:T(8,128)} fusion(f32[75,128,128]{2,1,0:T(8,128)} %bitcast.361, f32[75,64,128]{2,1,0:T(8,128)} %gather_fusion, pred[75]{0:T(512)(128)(4,1)S(1)} %compare_and_fusion), kind=kOutput, calls=%fused_computation.26 | convolution fusion | flops 944332800 | bytes 9830475 | tf_op jit(solution)/shard_map/hpk,pkl->hpl/dot_general | solution.py:23
  164.3 9.3 %fusion.4 = f32[25,64,3,128]{3,1,2,0:T(8,128)S(1)} fusion(f32[1,25,3,128,128]{4,3,2,1,0:T(8,128)} %param.57, f32[64,25,128]{2,0,1:T(8,128)S(1)} %get-tuple-element.280), kind=kOutput, calls=%fused_computation.8 | convolution fusion | flops 943718400 | bytes 8192000 | tf_op jit(solution)/shard_map/hil,iskl->hisk/dot_general | solution.py:29
  175.2 2.3 collective-permute-start.8
  177.5 2.4 fusion.12
  180.9 79.0 %all-reduce.5 = (f32[]{:T(128)}, f32[]{:T(128)}) all-reduce(f32[]{:T(128)S(6)} %add.306, f32[]{:T(128)} %get-tuple-element.279), channel_id=1, replica_groups=mesh['tm'=32,'region'=8] {'tm','region'}, use_global_device_ids=true, to_apply=%region_3.4 | all-reduce | flops 2 | bytes 16 | tf_op jit(solution)/shard_map/psum | solution.py:111
  263.2 2.5 collective-permute-start.11
  270.1 2.2 collective-permute-start.12
  273.6 2.8 collective-permute-done.12
  277.3 20.0 %reduce-scatter.7.cloned.1.call-done = f32[1,64,128]{2,1,0:T(8,128)} async-done(((f32[8,64,128]{2,1,0:T(8,128)}), f32[1,64,128]{2,1,0:T(8,128)}) %reduce-scatter.7.cloned.1.call-update) | async-done | bytes 32784 | tf_op jit(solution)/shard_map/reduce_scatter | solution.py:87
  304.0 2.9 collective-permute-start.13
  306.8 16.3 %all-gather.3 = f32[512,1,128]{2,1,0:T(1,128)S(1)} all-gather(f32[64,1,128]{2,1,0:T(1,128)S(1)} %bitcast.386), channel_id=5, replica_groups=mesh['tm'=32,'region'=8] {'region'}, dimensions={0}, use_global_device_ids=true | all-gather | bytes 294912 | tf_op jit(solution)/shard_map/all_gather | solution.py:118
  323.1 7.9 %fusion.20 = f32[75,64,128]{2,1,0:T(8,128)} fusion(f32[75,128,128]{2,1,0:T(8,128)} %bitcast.362, f32[75,64,128]{2,1,0:T(8,128)} %gather_fusion.1, pred[75]{0:T(512)(128)(4,1)S(1)} %compare_and_fusion), kind=kOutput, calls=%fused_computation.24 | convolution fusion | flops 944332800 | bytes 9830475 | tf_op jit(solution)/shard_map/hpk,pkl->hpl/dot_general | solution.py:23
  336.2 9.3 %fusion.2 = f32[25,64,3,128]{3,1,2,0:T(8,128)S(1)} fusion(f32[1,25,3,128,128]{4,3,2,1,0:T(8,128)} %param.57, f32[64,25,128]{2,0,1:T(8,128)S(1)} %get-tuple-element.274), kind=kOutput, calls=%fused_computation.6 | convolution fusion | flops 943718400 | bytes 8192000 | tf_op jit(solution)/shard_map/hil,iskl->hisk/dot_general | solution.py:29
  347.0 2.4 collective-permute-start.15
  349.5 2.4 fusion.10
  352.3 2.5 collective-permute-start.16
  356.3 2.2 collective-permute-start.17
  358.5 76.9 %all-reduce.4 = (f32[]{:T(128)}, f32[]{:T(128)}) all-reduce(f32[]{:T(128)S(6)} %add.319, f32[]{:T(128)} %get-tuple-element.273), channel_id=1, replica_groups=mesh['tm'=32,'region'=8] {'tm','region'}, use_global_device_ids=true, to_apply=%region_11.13 | all-reduce | flops 2 | bytes 16 | tf_op jit(solution)/shard_map/psum | solution.py:111
  441.5 3.3 collective-permute-start.19
  448.8 20.2 %reduce-scatter.9.cloned.1.call-done = f32[1,64,128]{2,1,0:T(8,128)} async-done(((f32[8,64,128]{2,1,0:T(8,128)}), f32[1,64,128]{2,1,0:T(8,128)}) %reduce-scatter.9.cloned.1.call-update) | async-done | bytes 32784 | tf_op jit(solution)/shard_map/reduce_scatter | solution.py:87
  470.4 2.2 multiply_reduce_fusion.1
  474.7 2.8 collective-permute-start.20
  477.6 16.6 %all-gather.4 = f32[512,1,128]{2,1,0:T(1,128)S(1)} all-gather(f32[64,1,128]{2,1,0:T(1,128)S(1)} %bitcast.387), channel_id=6, replica_groups=mesh['tm'=32,'region'=8] {'region'}, dimensions={0}, use_global_device_ids=true | all-gather | bytes 294912 | tf_op jit(solution)/shard_map/all_gather | solution.py:118
  494.1 7.9 %fusion.18 = f32[75,64,128]{2,1,0:T(8,128)} fusion(f32[75,128,128]{2,1,0:T(8,128)} %bitcast.363, f32[75,64,128]{2,1,0:T(8,128)} %gather_fusion.2, pred[75]{0:T(512)(128)(4,1)S(1)} %compare_and_fusion), kind=kOutput, calls=%fused_computation.22 | convolution fusion | flops 944332800 | bytes 9830475 | tf_op jit(solution)/shard_map/hpk,pkl->hpl/dot_general | solution.py:23
  506.1 2.2 multiply_reduce_fusion
  508.3 9.3 %fusion = f32[25,64,3,128]{3,1,2,0:T(8,128)S(1)} fusion(f32[1,25,3,128,128]{4,3,2,1,0:T(8,128)} %param.57, f32[64,25,128]{2,0,1:T(8,128)S(1)} %get-tuple-element.270), kind=kOutput, calls=%fused_computation.4 | convolution fusion | flops 943718400 | bytes 8192000 | tf_op jit(solution)/shard_map/hil,iskl->hisk/dot_general | solution.py:29
  519.1 2.3 collective-permute-start.23
  521.5 2.4 fusion.8
  524.3 2.5 collective-permute-start.24
  528.3 2.2 collective-permute-start.25
  530.6 76.9 %all-reduce.3 = (f32[]{:T(128)}, f32[]{:T(128)}) all-reduce(f32[]{:T(128)S(6)} %add.333, f32[]{:T(128)} %get-tuple-element.269), channel_id=1, replica_groups=mesh['tm'=32,'region'=8] {'tm','region'}, use_global_device_ids=true, to_apply=%region_19.21 | all-reduce | flops 2 | bytes 16 | tf_op jit(solution)/shard_map/psum | solution.py:111
  613.4 3.3 collective-permute-start.27
  620.6 20.4 %reduce-scatter.11.cloned.1.call-done = f32[1,64,128]{2,1,0:T(8,128)} async-done(((f32[8,64,128]{2,1,0:T(8,128)}), f32[1,64,128]{2,1,0:T(8,128)}) %reduce-scatter.11.cloned.1.call-update) | async-done | bytes 32784 | tf_op jit(solution)/shard_map/reduce_scatter | solution.py:87
  642.4 2.7 multiply_subtract_fusion
  647.2 2.8 collective-permute-start.22
  650.0 16.3 %all-gather.5 = f32[512,1,128]{2,1,0:T(1,128)S(1)} all-gather(f32[64,1,128]{2,1,0:T(1,128)S(1)} %bitcast.385), channel_id=7, replica_groups=mesh['tm'=32,'region'=8] {'region'}, dimensions={0}, use_global_device_ids=true | all-gather | bytes 294912 | tf_op jit(solution)/shard_map/all_gather | solution.py:118
  666.3 8.0 %fusion.16 = f32[75,64,128]{2,1,0:T(8,128)} fusion(f32[75,128,128]{2,1,0:T(8,128)} %bitcast.364, f32[75,64,128]{2,1,0:T(8,128)} %gather_fusion.3, pred[75]{0:T(512)(128)(4,1)S(1)} %compare_and_fusion), kind=kOutput, calls=%fused_computation.20 | convolution fusion | flops 944332800 | bytes 9830475 | tf_op jit(solution)/shard_map/hpk,pkl->hpl/dot_general | solution.py:23
  (211 shorter events, 83.6 us)
Async XLA Ops:
  7.2 33.0 %copy-start = (f32[64,1,3200]{2,1,0:T(1,128)S(1)}, f32[64,1,3200]{2,1,0:T(1,128)}, u32[]{:S(2)}) copy-start(f32[64,1,3200]{2,1,0:T(1,128)} %param.53) | copy-start | bytes 2457604
  7.2 106.6 %reduce-scatter.5.cloned.1.call-start = ((), (), s32[]{:S(2)}) async-start(), calls=%async_computation.4 | async-start | bytes 294912 | tf_op jit(solution)/shard_map/reduce_scatter | solution.py:87
  7.2 101.6 %collective-permute-start = (f32[128]{0:T(128)S(1)}, f32[128]{0:T(128)S(1)}, u32[]{:S(2)}, u32[]{:S(2)}) collective-permute-start(f32[128]{0:T(128)S(1)} %broadcast.305), channel_id=1, source_target_pairs={{8,0},{16,8},{24,16},{32,24},{40,32},{48,40},{56,48},{64,56},{72,6... | collective-permute-start | bytes 1544 | tf_op jit(solution)/shard_map/ppermute | solution.py:16
  9.5 19.9 %collective-permute-start.1 = (f32[128]{0:T(128)S(1)}, f32[128]{0:T(128)S(1)}, u32[]{:S(2)}, u32[]{:S(2)}) collective-permute-start(f32[128]{0:T(128)S(1)} %fusion.51), channel_id=1, source_target_pairs={{0,8},{8,0},{16,24},{24,16},{32,40},{40,32},{48,56},{56,48},{64,72... | collective-permute-start | bytes 1544 | tf_op jit(solution)/shard_map/ppermute | solution.py:100
  15.5 281.9 %reduce-scatter.7.cloned.1.call-start = ((), (), s32[]{:S(2)}) async-start(), calls=%async_computation.5 | async-start | bytes 294912 | tf_op jit(solution)/shard_map/reduce_scatter | solution.py:87
  25.5 2.5 copy-start.16
  25.5 3.7 copy-start.12
  25.5 3.8 copy-start.13
  27.9 8.0 %copy-start.11 = (f32[1,3200]{1,0:T(1,128)S(1)}, f32[1,3200]{1,0:T(1,128)}, u32[]{:S(2)}) copy-start(f32[1,3200]{1,0:T(1,128)} %param.54) | copy-start | bytes 38404
  29.4 4.1 collective-permute-start.2
  33.0 80.6 %copy-start.14 = (s32[1,128]{1,0:T(1,128)S(1)}, s32[1,128]{1,0:T(1,128)}, u32[]{:S(2)}) copy-start(s32[1,128]{1,0:T(1,128)} %param.61) | copy-start | bytes 1540
  33.5 3.6 collective-permute-start.3
  37.1 69.4 %collective-permute-start.4 = (f32[128]{0:T(128)S(1)}, f32[128]{0:T(128)S(1)}, u32[]{:S(2)}, u32[]{:S(2)}) collective-permute-start(f32[128]{0:T(128)S(1)} %add.302), channel_id=1, source_target_pairs={{0,64},{8,72},{16,80},{24,88},{32,96},{40,104},{48,112},{56,120},{... | collective-permute-start | bytes 1544 | tf_op jit(solution)/shard_map/ppermute | solution.py:100
  106.5 6.4 collective-permute-start.5
  115.8 47.2 %collective-permute-start.6 = (f32[128]{0:T(128)S(1)}, f32[128]{0:T(128)S(1)}, u32[]{:S(2)}, u32[]{:S(2)}) collective-permute-start(f32[128]{0:T(128)S(1)} %slice_bitcast_fusion.16), channel_id=1, source_target_pairs={{0,8},{8,16},{16,24},{24,32},{32,40},{40,48},{48,56},{56,64},{64,7... | collective-permute-start | bytes 1544 | tf_op jit(solution)/shard_map/ppermute | solution.py:16
  159.2 3.8 copy-start.2
  164.3 15.6 %copy-start.8 = (f32[64,25,128]{2,0,1:T(8,128)}, f32[64,25,128]{2,0,1:T(8,128)S(1)}, u32[]{:S(2)}) copy-start(f32[64,25,128]{2,0,1:T(8,128)S(1)} %get-tuple-element.280) | copy-start | bytes 2457604
  173.8 98.4 %collective-permute-start.7 = (f32[128]{0:T(128)S(1)}, f32[128]{0:T(128)S(1)}, u32[]{:S(2)}, u32[]{:S(2)}) collective-permute-start(f32[128]{0:T(128)S(1)} %slice_bitcast_fusion.15), channel_id=1, source_target_pairs={{8,0},{16,8},{24,16},{32,24},{40,32},{48,40},{56,48},{64,56},{72,6... | collective-permute-start | bytes 1544 | tf_op jit(solution)/shard_map/ppermute | solution.py:16
  175.2 5.2 collective-permute-start.8
  180.4 79.5 %collective-permute-start.9 = (f32[128]{0:T(128)S(1)}, f32[128]{0:T(128)S(1)}, u32[]{:S(2)}, u32[]{:S(2)}) collective-permute-start(f32[128]{0:T(128)S(1)} %add.314), channel_id=1, source_target_pairs={{0,16},{8,24},{16,0},{24,8},{32,48},{40,56},{48,32},{56,40},{64,80... | collective-permute-start | bytes 1544 | tf_op jit(solution)/shard_map/ppermute | solution.py:100
  180.9 96.3 %copy-start.15 = (s32[1,128]{1,0:T(1,128)S(1)}, s32[1,128]{1,0:T(1,128)}, u32[]{:S(2)}) copy-start(s32[1,128]{1,0:T(1,128)} %param.61) | copy-start | bytes 1540
  259.9 3.2 collective-permute-start.10
  263.2 6.9 collective-permute-start.11
  270.0 199.0 %reduce-scatter.9.cloned.1.call-start = ((), (), s32[]{:S(2)}) async-start(), calls=%async_computation.6 | async-start | bytes 294912 | tf_op jit(solution)/shard_map/reduce_scatter | solution.py:87
  270.1 6.4 collective-permute-start.12
  304.0 30.8 %collective-permute-start.13 = (f32[128]{0:T(128)S(1)}, f32[128]{0:T(128)S(1)}, u32[]{:S(2)}, u32[]{:S(2)}) collective-permute-start(f32[128]{0:T(128)S(1)} %slice_bitcast_fusion.14), channel_id=1, source_target_pairs={{0,8},{8,16},{16,24},{24,32},{32,40},{40,48},{48,56},{56,64},{64,7... | collective-permute-start | bytes 1544 | tf_op jit(solution)/shard_map/ppermute | solution.py:16
  331.0 4.1 copy-start.9
  336.2 15.7 %copy-start.7 = (f32[64,25,128]{2,0,1:T(8,128)}, f32[64,25,128]{2,0,1:T(8,128)S(1)}, u32[]{:S(2)}) copy-start(f32[64,25,128]{2,0,1:T(8,128)S(1)} %get-tuple-element.274) | copy-start | bytes 2457604
  345.7 99.1 %collective-permute-start.14 = (f32[128]{0:T(128)S(1)}, f32[128]{0:T(128)S(1)}, u32[]{:S(2)}, u32[]{:S(2)}) collective-permute-start(f32[128]{0:T(128)S(1)} %slice_bitcast_fusion.13), channel_id=1, source_target_pairs={{8,0},{16,8},{24,16},{32,24},{40,32},{48,40},{56,48},{64,56},{72,6... | collective-permute-start | bytes 1544 | tf_op jit(solution)/shard_map/ppermute | solution.py:16
  347.0 5.2 collective-permute-start.15
  352.3 4.0 collective-permute-start.16
  355.2 115.2 %copy-start.4 = (f32[64,25,128]{2,0,1:T(8,128)S(1)}, f32[64,25,128]{2,0,1:T(8,128)}, u32[]{:S(2)}) copy-start(f32[64,25,128]{2,0,1:T(8,128)} %copy-done.3) | copy-start | bytes 2457604
  356.3 80.5 %collective-permute-start.17 = (f32[128]{0:T(128)S(1)}, f32[128]{0:T(128)S(1)}, u32[]{:S(2)}, u32[]{:S(2)}) collective-permute-start(f32[128]{0:T(128)S(1)} %add.329), channel_id=1, source_target_pairs={{0,32},{8,40},{16,48},{24,56},{32,0},{40,8},{48,16},{56,24},{64,96... | collective-permute-start | bytes 1544 | tf_op jit(solution)/shard_map/ppermute | solution.py:100
  436.8 4.6 collective-permute-start.18
  441.4 199.6 %reduce-scatter.11.cloned.1.call-start = ((), (), s32[]{:S(2)}) async-start(), calls=%async_computation.7 | async-start | bytes 294912 | tf_op jit(solution)/shard_map/reduce_scatter | solution.py:87
  441.5 6.4 collective-permute-start.19
  474.7 31.0 %collective-permute-start.20 = (f32[128]{0:T(128)S(1)}, f32[128]{0:T(128)S(1)}, u32[]{:S(2)}, u32[]{:S(2)}) collective-permute-start(f32[128]{0:T(128)S(1)} %slice_bitcast_fusion.12), channel_id=1, source_target_pairs={{0,8},{8,16},{16,24},{24,32},{32,40},{40,48},{48,56},{56,64},{64,7... | collective-permute-start | bytes 1544 | tf_op jit(solution)/shard_map/ppermute | solution.py:16
  508.2 15.6 %copy-start.5 = (f32[64,25,128]{2,0,1:T(8,128)}, f32[64,25,128]{2,0,1:T(8,128)S(1)}, u32[]{:S(2)}) copy-start(f32[64,25,128]{2,0,1:T(8,128)S(1)} %get-tuple-element.270) | copy-start | bytes 2457604
  517.8 98.9 %collective-permute-start.21 = (f32[128]{0:T(128)S(1)}, f32[128]{0:T(128)S(1)}, u32[]{:S(2)}, u32[]{:S(2)}) collective-permute-start(f32[128]{0:T(128)S(1)} %slice_bitcast_fusion.11), channel_id=1, source_target_pairs={{8,0},{16,8},{24,16},{32,24},{40,32},{48,40},{56,48},{64,56},{72,6... | collective-permute-start | bytes 1544 | tf_op jit(solution)/shard_map/ppermute | solution.py:16
  519.1 5.2 collective-permute-start.23
  524.3 4.0 collective-permute-start.24
  528.3 80.5 %collective-permute-start.25 = (f32[128]{0:T(128)S(1)}, f32[128]{0:T(128)S(1)}, u32[]{:S(2)}, u32[]{:S(2)}) collective-permute-start(f32[128]{0:T(128)S(1)} %add.345), channel_id=1, source_target_pairs={{0,32},{8,40},{16,48},{24,56},{32,0},{40,8},{48,16},{56,24},{64,96... | collective-permute-start | bytes 1544 | tf_op jit(solution)/shard_map/ppermute | solution.py:100
  608.9 4.6 collective-permute-start.26
  613.4 6.4 collective-permute-start.27
  647.2 31.8 %collective-permute-start.22 = (f32[128]{0:T(128)S(1)}, f32[128]{0:T(128)S(1)}, u32[]{:S(2)}, u32[]{:S(2)}) collective-permute-start(f32[128]{0:T(128)S(1)} %slice_bitcast_fusion.10), channel_id=1, source_target_pairs={{0,8},{8,16},{16,24},{24,32},{32,40},{40,48},{48,56},{56,64},{64,7... | collective-permute-start | bytes 1544 | tf_op jit(solution)/shard_map/ppermute | solution.py:16
  666.3 8.4 %copy-start.10 = (f32[64,25,128]{2,0,1:T(8,128)S(1)}, f32[64,25,128]{2,0,1:T(8,128)}, u32[]{:S(2)}) copy-start(f32[64,25,128]{2,0,1:T(8,128)} %get-tuple-element.268) | copy-start | bytes 2457604
  675.2 4.1 copy-start.6
  679.3 2.4 copy-start.1
  (1 other events, 0.9 us)
Sparse Core Ops, SparseCore 0:
  15.6 35.0 reduce-scatter.4
  270.1 27.2 reduce-scatter.6
  441.5 27.4 reduce-scatter.8
  613.5 27.4 reduce-scatter.10
